TPU v7x, 32 devices: a whole 2x2x4 slice. The times are simulated.
32 devices in a mesh: seq: 16 (over z, x, core), fsdp: 2 (over y).
Axes of the slice: x: 2, y: 2, z: 4, core: 2. Of those that a mesh axis runs over, the one named last changes fastest.
Arguments:
- activations: bfloat16 [65536, 2048], P('seq', 'fsdp'), may hold values from -3 to 3
- mix_first: bfloat16 [256, 256], replicated, may hold values from -0.375 to 0.375
- twiddle: float32 [256, 256], P('seq'), may hold values from 0.4 to 2
- mix_second: bfloat16 [256, 256], replicated, may hold values from -0.375 to 0.375
- up_first: bfloat16 [8, 256, 256], P('fsdp'), may hold values from -0.375 to 0.375
- up_second: bfloat16 [8, 256, 1024], P('fsdp'), may hold values from -0.375 to 0.375
- down_first: bfloat16 [8, 1024, 256], P('fsdp'), may hold values from -0.1875 to 0.1875
- down_second: bfloat16 [8, 256, 256], P('fsdp'), may hold values from -0.375 to 0.375
- grad_out: bfloat16 [65536, 2048], P('seq', 'fsdp'), may hold values from -3 to 3
Outputs:
- output: bfloat16 [65536, 2048], P('seq', 'fsdp')
- grad_inputs: bfloat16 [65536, 2048], P('seq', 'fsdp')
- grad_up_first: float32 [8, 256, 256], P('fsdp')
- grad_up_second: float32 [8, 256, 1024], P('fsdp')
- grad_down_first: float32 [8, 1024, 256], P('fsdp')
- grad_down_second: float32 [8, 256, 256], P('fsdp')
All inputs are finite; a program needn't handle non-finite values.
Results may differ from a plain program's by a relative error of at most 0.01.
Values may be sent and summed in bfloat16 or wider, within the bound.
No kernel may reach another device: no remote copies, remote signals or barrier semaphores. Data moves between devices by JAX's collectives and lax.ppermute only.
A program may use at most 320 MiB of HBM per device.

v0:
```python
import jax
import jax.numpy as jnp
from jax import lax
from jax.sharding import PartitionSpec as P

NBLK = 8
root_two_pi = 0.7978845608028654
cubic_term = 0.044715


def gelu_value(values):
    inner = root_two_pi * (values + cubic_term * values * values * values)
    return 0.5 * values * (1.0 + jnp.tanh(inner))


def gelu_slope(values):
    inner = root_two_pi * (values + cubic_term * values * values * values)
    hyper = jnp.tanh(inner)
    return 0.5 * (1.0 + hyper) + 0.5 * values * (1.0 - hyper * hyper) * root_two_pi * (
        1.0 + 3.0 * cubic_term * values * values
    )


def product(form, left, right):
    return jnp.einsum(form, left, right, preferred_element_type=jnp.float32)


def column_pass(field, factor):
    result = product(
        "ajc,ai->ijc", lax.all_to_all(field, "seq", split_axis=1, concat_axis=0, tiled=True), factor
    ).astype(jnp.bfloat16)
    return lax.all_to_all(result, "seq", split_axis=0, concat_axis=1, tiled=True)


def shuffle_blocks(values):
    return lax.all_to_all(values, "fsdp", split_axis=2, concat_axis=1, tiled=True)


def spread_blocks(values):
    count, local_blocks, width = values.shape
    stride = width // NBLK
    received = shuffle_blocks(values)
    shaped = received.reshape(count, NBLK, local_blocks, stride)
    return jnp.transpose(shaped, (0, 2, 3, 1)).reshape(count, local_blocks, width)


def return_blocks(values):
    count, local_blocks, width = values.shape
    stride = width // NBLK
    parts = NBLK // local_blocks
    shaped = values.reshape(count, local_blocks, stride, parts, local_blocks)
    sending = jnp.transpose(shaped, (0, 1, 3, 4, 2)).reshape(count, local_blocks, width)
    received = shuffle_blocks(sending).reshape(count, NBLK, local_blocks, stride)
    return jnp.transpose(received, (0, 2, 1, 3)).reshape(count, local_blocks, width)


def blocks_layer(hidden, grad_out, up_first, up_second, down_first, down_second):
    count, channels = hidden.shape
    local_blocks, width = (up_first.shape[0], up_first.shape[1])
    hidden_three = hidden.reshape(count, local_blocks, width)
    up_mid = product("tkp,kpq->tkq", hidden_three, up_first).astype(jnp.bfloat16)
    up_perm = spread_blocks(up_mid)
    pre_act = product("tge,geo->tgo", up_perm, up_second)
    activated = gelu_value(pre_act).astype(jnp.bfloat16)
    down_mid = product("tgo,goq->tgq", activated, down_first).astype(jnp.bfloat16)
    down_perm = spread_blocks(down_mid)
    down_out = product("tge,geq->tgq", down_perm, down_second).reshape(count, channels)
    output = (hidden.astype(jnp.float32) + down_out).astype(jnp.bfloat16)
    grad_three = grad_out.reshape(count, local_blocks, width)
    sum_down_second = product("tge,tgq->geq", down_perm, grad_three)
    back_perm = product("tgq,geq->tge", grad_three, down_second).astype(jnp.bfloat16)
    back_mid = return_blocks(back_perm)
    sum_down_first = product("tgo,tgq->goq", activated, back_mid)
    grad_act = product("tgq,goq->tgo", back_mid, down_first)
    grad_pre = (grad_act * gelu_slope(pre_act)).astype(jnp.bfloat16)
    sum_up_second = product("tge,tgo->geo", up_perm, grad_pre)
    grad_perm = product("tgo,geo->tge", grad_pre, up_second).astype(jnp.bfloat16)
    grad_mid = return_blocks(grad_perm)
    sum_up_first = product("tkp,tkq->kpq", hidden_three, grad_mid)
    grad_inner = product("tkq,kpq->tkp", grad_mid, up_first).reshape(count, channels)
    grad_hidden = (grad_out.astype(jnp.float32) + grad_inner).astype(jnp.bfloat16)
    return (output, grad_hidden, (sum_up_first, sum_up_second, sum_down_first, sum_down_second))


def shards(
    activations,
    mix_first,
    twiddle,
    mix_second,
    up_first,
    up_second,
    down_first,
    down_second,
    grad_out,
):
    local_rows, local_channels = activations.shape
    block_rows = twiddle.shape[0]
    length = mix_first.shape[0]
    inputs_three = activations.reshape(block_rows, length, local_channels)
    first_pass = (product("abc,bj->ajc", inputs_three, mix_first) * twiddle[:, :, None]).astype(
        jnp.bfloat16
    )
    mixed = column_pass(first_pass, mix_second).reshape(local_rows, local_channels)
    inputs_float = activations.astype(jnp.float32)
    gating = jax.nn.sigmoid(inputs_float)
    mixed_float = mixed.astype(jnp.float32)
    hidden = (inputs_float + gating * mixed_float).astype(jnp.bfloat16)
    output, grad_hidden, grads = blocks_layer(
        hidden, grad_out, up_first, up_second, down_first, down_second
    )
    totals = lax.psum((grads[0], grads[1], grads[2], grads[3]), "seq")
    grad_float = grad_hidden.astype(jnp.float32)
    grad_mixed = (grad_float * gating).astype(jnp.bfloat16)
    back_rows = column_pass(grad_mixed.reshape(block_rows, length, local_channels), mix_second.T)
    twisted = (back_rows.astype(jnp.float32) * twiddle[:, :, None]).astype(jnp.bfloat16)
    mix_grad = product("ajc,bj->abc", twisted, mix_first).reshape(local_rows, local_channels)
    grad_inputs = (grad_float * (1.0 + gating * (1.0 - gating) * mixed_float) + mix_grad).astype(
        jnp.bfloat16
    )
    scale = 1.0 / length
    return (
        output,
        grad_inputs,
        totals[0] * scale,
        totals[1] * scale,
        totals[2] * scale,
        totals[3] * scale,
    )


def solution(mesh):
    in_specs = (
        P("seq", "fsdp"),
        P(),
        P("seq", None),
        P(),
        P("fsdp", None, None),
        P("fsdp", None, None),
        P("fsdp", None, None),
        P("fsdp", None, None),
        P("seq", "fsdp"),
    )
    out_specs = (
        P("seq", "fsdp"),
        P("seq", "fsdp"),
        P("fsdp", None, None),
        P("fsdp", None, None),
        P("fsdp", None, None),
        P("fsdp", None, None),
    )
    return jax.shard_map(shards, mesh=mesh, in_specs=in_specs, out_specs=out_specs, check_vma=False)
```

profile of v0, /device:TPU:0, one launch (start us, length us, event | category | flops | bytes accessed | tf_op | source)
XLA Modules:
  0.0 1738.0 jit_solution(1957139552533190147)
XLA Ops:
  7.2 9.3 fusion.17
  16.5 11.5 copy.130
  28.0 189.5 %all_to_all.114 = bf16[16,256,1024]{2,0,1:T(8,128)(2,1)} all-to-all(bf16[16,256,1024]{2,0,1:T(8,128)(2,1)} %copy.130), channel_id=1, replica_groups=mesh['seq'=16,'fsdp'=2] {'seq'}, dimensions={1} | all-to-all | bytes 16777216 | tf_op jit(solution)/shard_map/all_to_all | solution.py:30
  217.4 12.9 copy.132
  230.3 17.0 convert_bitcast_fusion.7
  247.3 12.3 copy.134
  265.5 9.2 convert_bitcast_fusion.4
  274.7 13.1 reshape.92
  287.8 11.6 copy.150
  299.4 12.2 copy.151
  311.6 104.5 %all-to-all-done.1 = bf16[256,16,1024]{2,1,0:T(8,128)(2,1)} async-done(((bf16[256,16,1024]{2,1,0:T(8,128)(2,1)}), bf16[256,16,1024]{2,1,0:T(8,128)(2,1)}, u32[]{:S(2)}, u32[]{:S(2)}) %all-to-all-start.1) | async-done | bytes 8388640 | tf_op jit(solution)/shard_map/all_to_all | solution.py:32
  416.1 7.0 all-to-all-start.4
  423.1 11.6 convert_bitcast_fusion.1
  434.6 7.2 copy.135
  447.7 8.7 fusion.10
  456.3 12.0 copy.186
  468.3 9.8 convert_bitcast_fusion.6
  478.1 14.6 copy.137
  492.7 24.1 %all-to-all-done.4 = bf16[4096,4,256]{0,1,2:T(4,128)(2,1)} async-done(((bf16[4096,4,256]{0,1,2:T(4,128)(2,1)}), bf16[4096,4,256]{0,1,2:T(4,128)(2,1)}, u32[]{:S(2)}, u32[]{:S(2)}) %all-to-all-start.4) | async-done | bytes 8388640 | tf_op jit(solution)/shard_map/all_to_all | solution.py:36
  516.8 7.2 all-to-all-start.2
  524.0 11.2 copy.152
  535.2 7.8 copy.153
  543.0 7.8 copy.154
  550.8 66.1 %all-to-all-done.2 = bf16[4096,4,256]{0,1,2:T(4,128)(2,1)} async-done(((bf16[4096,4,256]{0,1,2:T(4,128)(2,1)}), bf16[4096,4,256]{0,1,2:T(4,128)(2,1)}, u32[]{:S(2)}, u32[]{:S(2)}) %all-to-all-start.2) | async-done | bytes 8388640 | tf_op jit(solution)/shard_map/all_to_all | solution.py:36
  616.9 11.3 copy.138
  628.1 7.7 copy.139
  635.9 48.6 %multiply_convert_fusion = (bf16[4096,4,1024]{2,0,1:T(8,128)(2,1)}, f32[4,4096,1024]{2,1,0:T(8,128)}) fusion(bf16[4,256,1024]{2,1,0:T(8,128)(2,1)S(1)} %copy-done, bf16[4096,4,32,8]{0,2,1,3:T(8,128)(2,1)} %bitcast.185), kind=kOutput, calls=%fused_computation.10 | convolution fusion | flops 8740929536 | bytes 111149056 | tf_op jit(solution)/shard_map/tge,geo->tgo/dot_general | solution.py:25
  684.5 53.2 %fusion.6 = bf16[4096,4,1024]{2,0,1:T(8,128)(2,1)} fusion(f32[4,4096,1024]{2,1,0:T(8,128)} %get-tuple-element.11, bf16[4096,4,256]{0,2,1:T(8,128)(2,1)} %bitcast.183, bf16[4,1024,256]{2,1,0:T(8,128)(2,1)} %param.15), kind=kOutput, calls=%fused_computation.8 | convolution fusion | flops 8908701696 | bytes 111149056 | tf_op jit(solution)/shard_map/tgq,goq->tgo/dot_general | solution.py:25
  737.7 19.0 %convert_bitcast_fusion.3 = bf16[4096,4,256]{0,2,1:T(8,128)(2,1)} fusion(bf16[4096,4,1024]{2,0,1:T(8,128)(2,1)} %fusion.6, bf16[4,256,1024]{2,1,0:T(8,128)(2,1)S(1)} %copy-done), kind=kOutput, calls=%fused_computation.50 | convolution fusion | flops 8594128896 | bytes 44040192 | tf_op jit(solution)/shard_map/tgo,geo->tge/dot_general | solution.py:25
  756.7 13.1 reshape.96
  769.8 11.5 copy.156
  781.3 10.1 copy.157
  791.4 96.6 %all_to_all.115 = bf16[4096,4,256]{0,1,2:T(4,128)(2,1)} all-to-all(bf16[4096,4,256]{0,1,2:T(4,128)(2,1)S(1)} %copy.157), channel_id=1, replica_groups=mesh['seq'=16,'fsdp'=2] {'fsdp'}, dimensions={2} | all-to-all | bytes 16777216 | tf_op jit(solution)/shard_map/all_to_all | solution.py:36
  888.0 11.3 copy.158
  899.3 7.7 copy.159
  907.0 7.8 copy.160
  914.8 11.5 fusion.52
  926.3 17.4 %copy.162 = f32[4096,1024]{1,0:T(8,128)} copy(f32[4096,1024]{0,1:T(8,128)} %bitcast.164) | data formatting | bytes 33554432 | tf_op jit(solution)/shard_map/reshape | solution.py:80
  943.8 15.4 fusion.13
  959.1 11.3 copy.163
  970.5 35.0 %all-to-all-start.6 = ((bf16[16,256,1024]{2,0,1:T(8,128)(2,1)}), bf16[16,256,1024]{2,0,1:T(8,128)(2,1)}, u32[]{:S(2)}, u32[]{:S(2)}) async-start(bf16[16,256,1024]{2,0,1:T(8,128)(2,1)} %copy.163), calls=%async_computation.6 | async-start | bytes 16777216 | tf_op jit(solution)/shard_map/all_to_all | solution.py:30
  1005.5 17.1 convert_bitcast_fusion.5
  1022.6 14.6 copy.142
  1037.2 118.8 %all-to-all-done.6 = bf16[16,256,1024]{2,0,1:T(8,128)(2,1)} async-done(((bf16[16,256,1024]{2,0,1:T(8,128)(2,1)}), bf16[16,256,1024]{2,0,1:T(8,128)(2,1)}, u32[]{:S(2)}, u32[]{:S(2)}) %all-to-all-start.6) | async-done | bytes 8388640 | tf_op jit(solution)/shard_map/all_to_all | solution.py:30
  1156.0 7.2 all-to-all-start.3
  1163.2 12.8 copy.165
  1176.0 23.3 %convert_bitcast_fusion.2 = bf16[256,16,1024]{0,2,1:T(8,128)(2,1)} fusion(bf16[256,16,1024]{2,1,0:T(8,128)(2,1)} %bitcast.162, bf16[256,256]{1,0:T(8,128)(2,1)S(1)} %copy-done.10), kind=kOutput, calls=%fused_computation.49 | convolution fusion | flops 2151677952 | bytes 16908288 | tf_op jit(solution)/shard_map/ajc,ai->ijc/dot_general | solution.py:25
  1199.3 12.4 copy.167
  1211.7 45.2 %all-to-all-done.3 = bf16[4096,4,256]{0,1,2:T(4,128)(2,1)} async-done(((bf16[4096,4,256]{0,1,2:T(4,128)(2,1)}), bf16[4096,4,256]{0,1,2:T(4,128)(2,1)}, u32[]{:S(2)}, u32[]{:S(2)}) %all-to-all-start.3) | async-done | bytes 8388640 | tf_op jit(solution)/shard_map/all_to_all | solution.py:36
  1256.9 36.0 %all-to-all-start.7 = ((bf16[256,16,1024]{2,1,0:T(8,128)(2,1)}), bf16[256,16,1024]{2,1,0:T(8,128)(2,1)}, u32[]{:S(2)}, u32[]{:S(2)}) async-start(bf16[256,16,1024]{2,1,0:T(8,128)(2,1)} %copy.167), calls=%async_computation.7 | async-start | bytes 16777216 | tf_op jit(solution)/shard_map/all_to_all | solution.py:32
  1293.3 20.5 %fusion.51 = f32[4,1024,256]{2,1,0:T(8,128)} fusion(bf16[4096,4,1024]{2,0,1:T(8,128)(2,1)} %get-tuple-element.10, bf16[4096,4,256]{0,2,1:T(8,128)(2,1)} %bitcast.184), kind=kOutput, calls=%fused_computation.71 | convolution fusion | flops 8589934592 | bytes 46137344 | tf_op jit(solution)/shard_map/tgo,tgq->goq/dot_general | solution.py:25
  1313.9 26.3 %fusion.25 = f32[4,256,1024]{2,1,0:T(8,128)} fusion(bf16[4096,4,1024]{2,0,1:T(8,128)(2,1)} %fusion.6, bf16[4096,4,32,8]{0,2,1,3:T(8,128)(2,1)} %bitcast.186), kind=kOutput, calls=%fused_computation.41 | convolution fusion | flops 8589934592 | bytes 46137344 | tf_op jit(solution)/shard_map/tge,tgo->geo/dot_general | solution.py:25
  1340.2 11.3 copy.143
  1351.5 7.9 copy.144
  1359.3 12.3 fusion.18
  1371.6 6.9 fusion.50
  1379.6 15.1 fusion.23
  1394.7 17.5 %copy.148 = f32[4096,1024]{1,0:T(8,128)} copy(f32[4096,1024]{0,1:T(8,128)} %bitcast.163) | data formatting | bytes 33554432 | tf_op jit(solution)/shard_map/reshape | solution.py:67
  1412.2 12.0 add_convert_fusion.1
  1424.3 243.4 %all-reduce.3.cloned.1.call-done = (f32[4,256,256]{2,1,0:T(8,128)}, f32[4,256,1024]{2,1,0:T(8,128)}, f32[4,1024,256]{2,1,0:T(8,128)}, f32[4,256,256]{2,1,0:T(8,128)}) async-done(((f32[4,256,256]{2,1,0:T(8,128)}, f32[4,256,1024]{2,1,0:T(8,128)}, f32[4,1024,256]{2,1,0:T(8,128)}, f32[4,256,256]{2,1,0:T(8,128)}), (f32[4,256,256]{2,1,0:T(8,128)}, f32[4,256,1024]{2,1,0:T(8,128)}, f32[4,1024,256]{2,1,0:T(8,128)}, ...) | async-done | bytes 10485776 | tf_op jit(solution)/shard_map/psum | solution.py:111
  1678.3 11.4 convert_bitcast_fusion
  1689.7 6.6 copy.168
  1698.9 8.1 fusion.47
  1707.0 23.6 %fusion.12 = bf16[4096,1024]{1,0:T(8,128)(2,1)} fusion(f32[16,1024,256]{1,2,0:T(8,128)} %fusion.47, f32[16,16,16,1024]{3,2,1,0:T(8,128)} %copy-done.2, bf16[4096,1024]{1,0:T(8,128)(2,1)S(1)} %bitcast.159, f32[4096,1024]{1,0:T(8,128)} %copy.162, bf16[4096,1024]{1,0:T(8,128)(2,1)} %param.17), kind=kLoop, calls=%fused_computation.21 | loop fusion | flops 62914560 | bytes 75497472 | tf_op jit(solution)/shard_map/convert_element_type | solution.py:117
  (49 shorter events, 26.5 us)
Async XLA Ops:
  7.2 628.7 %copy-start = (bf16[4,256,1024]{2,1,0:T(8,128)(2,1)S(1)}, bf16[4,256,1024]{2,1,0:T(8,128)(2,1)}, u32[]{:S(2)}) copy-start(bf16[4,256,1024]{2,1,0:T(8,128)(2,1)} %param.14) | copy-start | bytes 6291460
  217.4 12.9 copy-start.9
  259.6 5.9 copy-start.6
  259.6 156.5 %all-to-all-start.1 = ((bf16[256,16,1024]{2,1,0:T(8,128)(2,1)}), bf16[256,16,1024]{2,1,0:T(8,128)(2,1)}, u32[]{:S(2)}, u32[]{:S(2)}) async-start(bf16[256,16,1024]{2,1,0:T(8,128)(2,1)} %copy.134), calls=%async_computation.1 | async-start | bytes 16777216 | tf_op jit(solution)/shard_map/all_to_all | solution.py:32
  416.1 100.7 %all-to-all-start.4 = ((bf16[4096,4,256]{0,1,2:T(4,128)(2,1)}), bf16[4096,4,256]{0,1,2:T(4,128)(2,1)}, u32[]{:S(2)}, u32[]{:S(2)}) async-start(bf16[4096,4,256]{0,1,2:T(4,128)(2,1)} %copy.151), calls=%async_computation.4 | async-start | bytes 16777216 | tf_op jit(solution)/shard_map/all_to_all | solution.py:36
  423.0 24.6 %slice-start = ((s8[8388608]{0:T(1024)(128)(4,1)}), s8[4194304]{0:T(1024)(128)(4,1)S(1)}, s32[]{:S(2)}) async-start(s8[8388608]{0:T(1024)(128)(4,1)} %bitcast.156), calls=%async_computation.9 | async-start | bytes 8388608
  434.6 13.0 slice-start.1
  441.9 5.8 copy-start.2
  456.3 12.0 copy-start.4
  516.8 100.1 %all-to-all-start.2 = ((bf16[4096,4,256]{0,1,2:T(4,128)(2,1)}), bf16[4096,4,256]{0,1,2:T(4,128)(2,1)}, u32[]{:S(2)}, u32[]{:S(2)}) async-start(bf16[4096,4,256]{0,1,2:T(4,128)(2,1)} %copy.137), calls=%async_computation.2 | async-start | bytes 16777216 | tf_op jit(solution)/shard_map/all_to_all | solution.py:36
  907.0 7.8 copy-start.5
  970.5 35.0 %copy-start.12 = (bf16[4,1024,256]{2,1,0:T(8,128)(2,1)S(1)}, bf16[4,1024,256]{2,1,0:T(8,128)(2,1)}, u32[]{:S(2)}) copy-start(bf16[4,1024,256]{2,1,0:T(8,128)(2,1)} %param.15) | copy-start | bytes 6291460
  970.5 185.5 %all-to-all-start.6 = ((bf16[16,256,1024]{2,0,1:T(8,128)(2,1)}), bf16[16,256,1024]{2,0,1:T(8,128)(2,1)}, u32[]{:S(2)}, u32[]{:S(2)}) async-start(bf16[16,256,1024]{2,0,1:T(8,128)(2,1)} %copy.163), calls=%async_computation.6 | async-start | bytes 16777216 | tf_op jit(solution)/shard_map/all_to_all | solution.py:30
  1156.0 100.9 %all-to-all-start.3 = ((bf16[4096,4,256]{0,1,2:T(4,128)(2,1)}), bf16[4096,4,256]{0,1,2:T(4,128)(2,1)}, u32[]{:S(2)}, u32[]{:S(2)}) async-start(bf16[4096,4,256]{0,1,2:T(4,128)(2,1)} %copy.142), calls=%async_computation.3 | async-start | bytes 16777216 | tf_op jit(solution)/shard_map/all_to_all | solution.py:36
  1163.2 12.8 copy-start.10
  1256.9 421.4 %all-to-all-start.7 = ((bf16[256,16,1024]{2,1,0:T(8,128)(2,1)}), bf16[256,16,1024]{2,1,0:T(8,128)(2,1)}, u32[]{:S(2)}, u32[]{:S(2)}) async-start(bf16[256,16,1024]{2,1,0:T(8,128)(2,1)} %copy.167), calls=%async_computation.7 | async-start | bytes 16777216 | tf_op jit(solution)/shard_map/all_to_all | solution.py:32
  1292.9 374.7 %all-reduce.3.cloned.1.call-start = ((), (), s32[]{:S(2)}) async-start(), calls=%async_computation.8 | async-start | bytes 20971520 | tf_op jit(solution)/shard_map/psum | solution.py:111
  1351.5 20.1 %slice-start.4 = ((s8[8388608]{0:T(1024)(128)(4,1)}), s8[4194304]{0:T(1024)(128)(4,1)S(1)}, s32[]{:S(2)}) async-start(s8[8388608]{0:T(1024)(128)(4,1)} %bitcast.166), calls=%async_computation.13 | async-start | bytes 8388608
  1359.3 12.3 slice-start.5
  1378.5 1.0 copy-start.7
  1667.6 8.3 copy-start.3
  1689.7 6.6 copy-start.11
  1696.3 2.6 copy-start.8
  1696.3 10.7 slice-start.2
  1698.9 8.1 slice-start.3
  1707.0 23.6 %copy-start.1 = (bf16[4,256,1024]{2,1,0:T(8,128)(2,1)S(1)}, bf16[4,256,1024]{2,1,0:T(8,128)(2,1)}, u32[]{:S(2)}) copy-start(bf16[4,256,1024]{2,1,0:T(8,128)(2,1)} %param.14) | copy-start | bytes 6291460
Sparse Core Ops, SparseCore 0:
  1378.7 288.8 all-reduce.2
where the time goes:
time: 1750 us; the launch traced here: 1740 us
  waiting for transfers between devices  602 us (34%)
  local copies, waits for them, and re-layouts  333 us (19%)
  matrix products  307 us (18%)
  blocking collectives  286 us (16%)
  starting transfers between devices  98.6 us (6%)
  other arithmetic  95.9 us (5%)
    dot_general x16, matrix products, product(): return jnp.einsum(form, left, right, preferred_element_type=jnp.float32)  307 us
    psum x1, waiting for transfers between devices, shards(): totals = lax.psum((grads[0], grads[1], grads[2], grads[3]), 'seq')  243 us
    all_to_all x1, blocking collectives, column_pass(): lax.all_to_all(field, 'seq', split_axis=1, concat_axis=0, tiled=True)  189 us
    all_to_all x3, waiting for transfers between devices, shuffle_blocks(): lax.all_to_all(values, 'fsdp', split_axis=2, concat_axis=1, tiled=True)  135 us
    all_to_all x1, waiting for transfers between devices, column_pass(): lax.all_to_all(field, 'seq', split_axis=1, concat_axis=0, tiled=True)  119 us
    all_to_all x2, waiting for transfers between devices, column_pass(): lax.all_to_all(result, 'seq', split_axis=0, concat_axis=1, tiled=True)  104 us
    all_to_all x1, blocking collectives, shuffle_blocks(): lax.all_to_all(values, 'fsdp', split_axis=2, concat_axis=1, tiled=True)  96.6 us
    all_to_all x8, local copies, waits for them, and re-layouts, shuffle_blocks(): lax.all_to_all(values, 'fsdp', split_axis=2, concat_axis=1, tiled=True)  76.1 us
  transfers between devices with their start and end apart: 7, of which 6 were waited for; matrix products, arithmetic and copies ran while one was open for 21% of the time, Pallas kernels for 0%

commit v1 on v0

--- a/solution.py
+++ b/solution.py
@@ -33,7 +33,15 @@
 
 
 def shuffle_blocks(values):
-    return lax.all_to_all(values, "fsdp", split_axis=2, concat_axis=1, tiled=True)
+    return jnp.concatenate(
+        lax.all_to_all(
+            jnp.stack(jnp.split(values, lax.psum(1, "fsdp"), axis=2), 0),
+            axis_name="fsdp",
+            split_axis=0,
+            concat_axis=0,
+        ),
+        axis=1,
+    )
 
 
 def spread_blocks(values):

time: 1750 us -> 1730 us (0.989)
  local copies, waits for them, and re-layouts: 333 us -> 250 us
  waiting for transfers between devices: 602 us -> 634 us
  other arithmetic: 95.9 us -> 120 us
    all_to_all x8 -> x0, local copies, waits for them, and re-layouts: 76.1 us -> none  [shuffle_blocks(): lax.all_to_all(values, 'fsdp', split_axis=2, concat_axis=1, tiled=True)]
    convert_element_type x2 -> x0, local copies, waits for them, and re-layouts: 29.2 us -> none  [the longest x1 14.6 us: blocks_layer(): product('tgo,goq->tgq', activated, down_first).astype(jnp.bfloat16)]
    another operation x0 -> x4, other arithmetic: none -> 24.8 us  [shuffle_blocks(): jnp.stack(jnp.split(values, lax.psum(1, 'fsdp'), axis=2), 0)]
    all_to_all x3, waiting for transfers between devices: 135 us -> 158 us  [shuffle_blocks(): lax.all_to_all(jnp.stack(jnp.split(values, lax.psum(1, 'fsdp'), axis=2),...]
    another operation x0 -> x4, local copies, waits for them, and re-layouts: none -> 20.4 us  [shuffle_blocks(): jnp.stack(jnp.split(values, lax.psum(1, 'fsdp'), axis=2), 0)]
  transfers between devices with their start and end apart: 7 -> 7, of which waited for: 6 -> 6; matrix products, arithmetic and copies ran while one was open for 21% -> 19% of each run, Pallas kernels for 0% -> 0%
where the time goes in v1:
time: 1730 us; the launch traced here: 1720 us
  waiting for transfers between devices  634 us (37%)
  matrix products  309 us (18%)
  blocking collectives  293 us (17%)
  local copies, waits for them, and re-layouts  250 us (14%)
  other arithmetic  120 us (7%)
  starting transfers between devices  98.4 us (6%)
    dot_general x16, matrix products, product(): return jnp.einsum(form, left, right, preferred_element_type=jnp.float32)  309 us
    psum x1, waiting for transfers between devices, shards(): totals = lax.psum((grads[0], grads[1], grads[2], grads[3]), 'seq')  249 us
    all_to_all x1, blocking collectives, column_pass(): lax.all_to_all(field, 'seq', split_axis=1, concat_axis=0, tiled=True)  189 us
    all_to_all x3, waiting for transfers between devices, shuffle_blocks(): lax.all_to_all(jnp.stack(jnp.split(values, lax.psum(1, 'fsdp'), axis=2),...  158 us
    all_to_all x1, waiting for transfers between devices, column_pass(): lax.all_to_all(field, 'seq', split_axis=1, concat_axis=0, tiled=True)  122 us
    all_to_all x2, waiting for transfers between devices, column_pass(): lax.all_to_all(result, 'seq', split_axis=0, concat_axis=1, tiled=True)  105 us
    all_to_all x1, blocking collectives, shuffle_blocks(): lax.all_to_all(jnp.stack(jnp.split(values, lax.psum(1, 'fsdp'), axis=2),...  103 us
    reshape x4, local copies, waits for them, and re-layouts, return_blocks(): shaped = values.reshape(count, local_blocks, stride, parts, local_blocks)  49.3 us
  transfers between devices with their start and end apart: 7, of which 6 were waited for; matrix products, arithmetic and copies ran while one was open for 19% of the time, Pallas kernels for 0%

profile of v1, /device:TPU:0, one launch (start us, length us, event | category | flops | bytes accessed | tf_op | source)
XLA Modules:
  0.0 1718.8 jit_solution(11657792446542434405)
XLA Ops:
  7.2 9.3 fusion.17
  16.5 11.5 copy.126
  28.0 189.5 %all_to_all.74 = bf16[16,256,1024]{2,0,1:T(8,128)(2,1)} all-to-all(bf16[16,256,1024]{2,0,1:T(8,128)(2,1)} %copy.126), channel_id=1, replica_groups=mesh['seq'=16,'fsdp'=2] {'seq'}, dimensions={1} | all-to-all | bytes 16777216 | tf_op jit(solution)/shard_map/all_to_all | solution.py:30
  217.4 12.9 copy.128
  230.3 16.8 convert_bitcast_fusion.7
  247.1 12.3 copy.130
  259.4 5.9 all-to-all-start.1
  265.3 9.2 convert_bitcast_fusion.4
  274.4 13.1 reshape.88
  287.5 11.6 copy.142
  299.2 5.2 slice_bitcast_fusion.3
  304.3 6.2 pad_maximum_fusion.2
  310.5 105.3 %all-to-all-done.1 = bf16[256,16,1024]{2,1,0:T(8,128)(2,1)} async-done(((bf16[256,16,1024]{2,1,0:T(8,128)(2,1)}), bf16[256,16,1024]{2,1,0:T(8,128)(2,1)}, u32[]{:S(2)}, u32[]{:S(2)}) %all-to-all-start.1) | async-done | bytes 8388640 | tf_op jit(solution)/shard_map/all_to_all | solution.py:32
  415.8 7.0 all-to-all-start.4
  422.8 11.6 convert_bitcast_fusion.1
  434.4 7.3 copy.131
  441.7 5.7 copy-done.2
  447.5 8.7 fusion.10
  456.1 12.0 copy.172
  468.1 9.8 convert_bitcast_fusion.6
  477.9 5.1 slice_bitcast_fusion.7
  483.0 6.2 pad_maximum_fusion
  489.2 27.3 %all-to-all-done.4 = bf16[2,4096,4,128]{1,3,2,0:T(8,128)(2,1)} async-done(((bf16[2,4096,4,128]{1,3,2,0:T(8,128)(2,1)}), bf16[2,4096,4,128]{1,3,2,0:T(8,128)(2,1)}, u32[]{:S(2)}, u32[]{:S(2)}) %all-to-all-start.4) | async-done | bytes 8388640 | tf_op jit(solution)/shard_map/all_to_all | solution.py:37
  516.5 7.0 all-to-all-start.2
  523.5 7.8 copy.143
  531.3 85.1 %all-to-all-done.2 = bf16[2,4096,4,128]{3,1,2,0:T(8,128)(2,1)} async-done(((bf16[2,4096,4,128]{3,1,2,0:T(8,128)(2,1)}), bf16[2,4096,4,128]{3,1,2,0:T(8,128)(2,1)}, u32[]{:S(2)}, u32[]{:S(2)}) %all-to-all-start.2) | async-done | bytes 8388640 | tf_op jit(solution)/shard_map/all_to_all | solution.py:37
  616.4 12.5 copy.133
  628.9 48.2 %multiply_convert_fusion = (bf16[4096,4,1024]{2,0,1:T(8,128)(2,1)}, f32[4,4096,1024]{2,1,0:T(8,128)}) fusion(bf16[4,256,1024]{2,1,0:T(8,128)(2,1)S(1)} %copy-done, bf16[4096,4,32,8]{0,2,1,3:T(8,128)(2,1)} %bitcast.188), kind=kOutput, calls=%fused_computation.10 | convolution fusion | flops 8740929536 | bytes 111149056 | tf_op jit(solution)/shard_map/tge,geo->tgo/dot_general | solution.py:25
  677.1 53.2 %fusion.6 = bf16[4096,4,1024]{2,0,1:T(8,128)(2,1)} fusion(f32[4,4096,1024]{2,1,0:T(8,128)} %get-tuple-element.19, bf16[4096,4,256]{0,2,1:T(8,128)(2,1)} %bitcast.186, bf16[4,1024,256]{2,1,0:T(8,128)(2,1)} %param.15), kind=kOutput, calls=%fused_computation.8 | convolution fusion | flops 8908701696 | bytes 111149056 | tf_op jit(solution)/shard_map/tgq,goq->tgo/dot_general | solution.py:25
  730.3 19.0 %convert_bitcast_fusion.3 = bf16[4096,4,256]{0,2,1:T(8,128)(2,1)} fusion(bf16[4096,4,1024]{2,0,1:T(8,128)(2,1)} %fusion.6, bf16[4,256,1024]{2,1,0:T(8,128)(2,1)S(1)} %copy-done), kind=kOutput, calls=%fused_computation.54 | convolution fusion | flops 8594128896 | bytes 44040192 | tf_op jit(solution)/shard_map/tgo,geo->tge/dot_general | solution.py:25
  749.3 13.1 reshape.92
  762.4 11.5 copy.145
  773.9 5.2 slice_bitcast_fusion.1
  779.1 6.2 pad_maximum_fusion.3
  785.3 103.4 %all_to_all.75 = bf16[2,4096,4,128]{1,3,2,0:T(8,128)(2,1)} all-to-all(bf16[2,4096,4,128]{1,3,2,0:T(8,128)(2,1)} %pad_maximum_fusion.3), channel_id=1, replica_groups=mesh['seq'=16,'fsdp'=2] {'fsdp'}, dimensions={0} | all-to-all | bytes 16777216 | tf_op jit(solution)/shard_map/all_to_all | solution.py:37
  888.7 7.8 copy.146
  896.5 11.5 fusion.52
  908.0 17.4 %copy.148 = f32[4096,1024]{1,0:T(8,128)} copy(f32[4096,1024]{0,1:T(8,128)} %bitcast.174) | data formatting | bytes 33554432 | tf_op jit(solution)/shard_map/reshape | solution.py:88
  925.5 15.0 fusion.13
  940.5 11.3 copy.149
  951.8 35.0 %all-to-all-start.6 = ((bf16[16,256,1024]{2,0,1:T(8,128)(2,1)}), bf16[16,256,1024]{2,0,1:T(8,128)(2,1)}, u32[]{:S(2)}, u32[]{:S(2)}) async-start(bf16[16,256,1024]{2,0,1:T(8,128)(2,1)} %copy.149), calls=%async_computation.6 | async-start | bytes 16777216 | tf_op jit(solution)/shard_map/all_to_all | solution.py:30
  986.8 17.1 convert_bitcast_fusion.5
  1003.9 5.1 slice_bitcast_fusion.5
  1008.9 6.2 pad_maximum_fusion.1
  1015.1 122.2 %all-to-all-done.6 = bf16[16,256,1024]{2,0,1:T(8,128)(2,1)} async-done(((bf16[16,256,1024]{2,0,1:T(8,128)(2,1)}), bf16[16,256,1024]{2,0,1:T(8,128)(2,1)}, u32[]{:S(2)}, u32[]{:S(2)}) %all-to-all-start.6) | async-done | bytes 8388640 | tf_op jit(solution)/shard_map/all_to_all | solution.py:30
  1137.3 7.2 all-to-all-start.3
  1144.5 12.8 copy.151
  1157.3 23.3 %convert_bitcast_fusion.2 = bf16[256,16,1024]{0,2,1:T(8,128)(2,1)} fusion(bf16[256,16,1024]{2,1,0:T(8,128)(2,1)} %bitcast.172, bf16[256,256]{1,0:T(8,128)(2,1)S(1)} %copy-done.10), kind=kOutput, calls=%fused_computation.53 | convolution fusion | flops 2151677952 | bytes 16908288 | tf_op jit(solution)/shard_map/ajc,ai->ijc/dot_general | solution.py:25
  1180.6 12.4 copy.153
  1193.0 45.2 %all-to-all-done.3 = bf16[2,4096,4,128]{3,1,2,0:T(8,128)(2,1)} async-done(((bf16[2,4096,4,128]{3,1,2,0:T(8,128)(2,1)}), bf16[2,4096,4,128]{3,1,2,0:T(8,128)(2,1)}, u32[]{:S(2)}, u32[]{:S(2)}) %all-to-all-start.3) | async-done | bytes 8388640 | tf_op jit(solution)/shard_map/all_to_all | solution.py:37
  1238.2 36.0 %all-to-all-start.7 = ((bf16[256,16,1024]{2,1,0:T(8,128)(2,1)}), bf16[256,16,1024]{2,1,0:T(8,128)(2,1)}, u32[]{:S(2)}, u32[]{:S(2)}) async-start(bf16[256,16,1024]{2,1,0:T(8,128)(2,1)} %copy.153), calls=%async_computation.7 | async-start | bytes 16777216 | tf_op jit(solution)/shard_map/all_to_all | solution.py:32
  1274.7 20.5 %fusion.51 = f32[4,1024,256]{2,1,0:T(8,128)} fusion(bf16[4096,4,1024]{2,0,1:T(8,128)(2,1)} %get-tuple-element.18, bf16[4096,4,256]{0,2,1:T(8,128)(2,1)} %bitcast.187), kind=kOutput, calls=%fused_computation.83 | convolution fusion | flops 8589934592 | bytes 46137344 | tf_op jit(solution)/shard_map/tgo,tgq->goq/dot_general | solution.py:25
  1295.2 26.2 %fusion.25 = f32[4,256,1024]{2,1,0:T(8,128)} fusion(bf16[4096,4,1024]{2,0,1:T(8,128)(2,1)} %fusion.6, bf16[4096,4,32,8]{0,2,1,3:T(8,128)(2,1)} %bitcast.189), kind=kOutput, calls=%fused_computation.45 | convolution fusion | flops 8589934592 | bytes 46137344 | tf_op jit(solution)/shard_map/tge,tgo->geo/dot_general | solution.py:25
  1321.4 11.6 copy.136
  1332.9 12.1 fusion.18
  1345.0 9.1 fusion.50
  1355.2 15.4 fusion.23
  1370.5 17.5 %copy.140 = f32[4096,1024]{1,0:T(8,128)} copy(f32[4096,1024]{0,1:T(8,128)} %bitcast.173) | data formatting | bytes 33554432 | tf_op jit(solution)/shard_map/reshape | solution.py:75
  1388.1 12.0 add_convert_fusion.1
  1400.1 248.8 %all-reduce.3.cloned.1.call-done = (f32[4,256,256]{2,1,0:T(8,128)}, f32[4,256,1024]{2,1,0:T(8,128)}, f32[4,1024,256]{2,1,0:T(8,128)}, f32[4,256,256]{2,1,0:T(8,128)}) async-done(((f32[4,256,256]{2,1,0:T(8,128)}, f32[4,256,1024]{2,1,0:T(8,128)}, f32[4,1024,256]{2,1,0:T(8,128)}, f32[4,256,256]{2,1,0:T(8,128)}), (f32[4,256,256]{2,1,0:T(8,128)}, f32[4,256,1024]{2,1,0:T(8,128)}, f32[4,1024,256]{2,1,0:T(8,128)}, ...) | async-done | bytes 10485776 | tf_op jit(solution)/shard_map/psum | solution.py:119
  1659.6 11.4 convert_bitcast_fusion
  1671.0 6.6 copy.154
  1680.0 8.1 fusion.47
  1688.1 23.6 %fusion.12 = bf16[4096,1024]{1,0:T(8,128)(2,1)} fusion(f32[16,1024,256]{1,2,0:T(8,128)} %fusion.47, f32[16,16,16,1024]{3,2,1,0:T(8,128)} %copy-done.2, bf16[4096,1024]{1,0:T(8,128)(2,1)S(1)} %bitcast.169, f32[4096,1024]{1,0:T(8,128)} %copy.148, bf16[4096,1024]{1,0:T(8,128)(2,1)} %param.17), kind=kLoop, calls=%fused_computation.21 | loop fusion | flops 62914560 | bytes 75497472 | tf_op jit(solution)/shard_map/convert_element_type | solution.py:125
  (42 shorter events, 14.6 us)
Async XLA Ops:
  7.2 621.7 %copy-start = (bf16[4,256,1024]{2,1,0:T(8,128)(2,1)S(1)}, bf16[4,256,1024]{2,1,0:T(8,128)(2,1)}, u32[]{:S(2)}) copy-start(bf16[4,256,1024]{2,1,0:T(8,128)(2,1)} %param.14) | copy-start | bytes 6291460
  217.4 12.9 copy-start.9
  259.4 5.9 copy-start.6
  259.4 156.5 %all-to-all-start.1 = ((bf16[256,16,1024]{2,1,0:T(8,128)(2,1)}), bf16[256,16,1024]{2,1,0:T(8,128)(2,1)}, u32[]{:S(2)}, u32[]{:S(2)}) async-start(bf16[256,16,1024]{2,1,0:T(8,128)(2,1)} %copy.130), calls=%async_computation.1 | async-start | bytes 16777216 | tf_op jit(solution)/shard_map/all_to_all | solution.py:32
  415.8 100.7 %all-to-all-start.4 = ((bf16[2,4096,4,128]{1,3,2,0:T(8,128)(2,1)}), bf16[2,4096,4,128]{1,3,2,0:T(8,128)(2,1)}, u32[]{:S(2)}, u32[]{:S(2)}) async-start(bf16[2,4096,4,128]{1,3,2,0:T(8,128)(2,1)} %pad_maximum_fusion.2), calls=%async_computation.4 | async-start | bytes 16777216 | tf_op jit(solution)/shard_map/all_to_all | solution.py:37
  422.8 24.6 %slice-start = ((s8[8388608]{0:T(1024)(128)(4,1)}), s8[4194304]{0:T(1024)(128)(4,1)S(1)}, s32[]{:S(2)}) async-start(s8[8388608]{0:T(1024)(128)(4,1)} %bitcast.166), calls=%async_computation.9 | async-start | bytes 8388608
  434.4 13.1 slice-start.1
  441.7 5.8 copy-start.2
  456.1 12.0 copy-start.4
  516.5 99.9 %all-to-all-start.2 = ((bf16[2,4096,4,128]{3,1,2,0:T(8,128)(2,1)}), bf16[2,4096,4,128]{3,1,2,0:T(8,128)(2,1)}, u32[]{:S(2)}, u32[]{:S(2)}) async-start(bf16[2,4096,4,128]{3,1,2,0:T(8,128)(2,1)} %pad_maximum_fusion), calls=%async_computation.2 | async-start | bytes 16777216 | tf_op jit(solution)/shard_map/all_to_all | solution.py:37
  888.7 7.8 copy-start.5
  951.8 35.0 %copy-start.12 = (bf16[4,1024,256]{2,1,0:T(8,128)(2,1)S(1)}, bf16[4,1024,256]{2,1,0:T(8,128)(2,1)}, u32[]{:S(2)}) copy-start(bf16[4,1024,256]{2,1,0:T(8,128)(2,1)} %param.15) | copy-start | bytes 6291460
  951.8 185.5 %all-to-all-start.6 = ((bf16[16,256,1024]{2,0,1:T(8,128)(2,1)}), bf16[16,256,1024]{2,0,1:T(8,128)(2,1)}, u32[]{:S(2)}, u32[]{:S(2)}) async-start(bf16[16,256,1024]{2,0,1:T(8,128)(2,1)} %copy.149), calls=%async_computation.6 | async-start | bytes 16777216 | tf_op jit(solution)/shard_map/all_to_all | solution.py:30
  1137.3 100.9 %all-to-all-start.3 = ((bf16[2,4096,4,128]{3,1,2,0:T(8,128)(2,1)}), bf16[2,4096,4,128]{3,1,2,0:T(8,128)(2,1)}, u32[]{:S(2)}, u32[]{:S(2)}) async-start(bf16[2,4096,4,128]{3,1,2,0:T(8,128)(2,1)} %pad_maximum_fusion.1), calls=%async_computation.3 | async-start | bytes 16777216 | tf_op jit(solution)/shard_map/all_to_all | solution.py:37
  1144.5 12.8 copy-start.10
  1238.2 421.4 %all-to-all-start.7 = ((bf16[256,16,1024]{2,1,0:T(8,128)(2,1)}), bf16[256,16,1024]{2,1,0:T(8,128)(2,1)}, u32[]{:S(2)}, u32[]{:S(2)}) async-start(bf16[256,16,1024]{2,1,0:T(8,128)(2,1)} %copy.153), calls=%async_computation.7 | async-start | bytes 16777216 | tf_op jit(solution)/shard_map/all_to_all | solution.py:32
  1274.2 374.7 %all-reduce.3.cloned.1.call-start = ((), (), s32[]{:S(2)}) async-start(), calls=%async_computation.8 | async-start | bytes 20971520 | tf_op jit(solution)/shard_map/psum | solution.py:119
  1354.1 1.0 copy-start.7
  1648.9 8.3 copy-start.3
  1671.0 6.6 copy-start.11
  1677.6 2.4 copy-start.8
  1677.6 10.5 slice-start.2
  1680.0 8.1 slice-start.3
  1688.1 23.6 %copy-start.1 = (bf16[4,256,1024]{2,1,0:T(8,128)(2,1)S(1)}, bf16[4,256,1024]{2,1,0:T(8,128)(2,1)}, u32[]{:S(2)}) copy-start(bf16[4,256,1024]{2,1,0:T(8,128)(2,1)} %param.14) | copy-start | bytes 6291460
Sparse Core Ops, SparseCore 0:
  1354.3 294.6 all-reduce.2
